TPU v7x, 32 devices: a whole 2x2x4 slice. The times are simulated.
32 devices in a mesh: dp: 4 (over x, core), fsdp: 8 (over z, y).
Axes of the slice: x: 2, y: 2, z: 4, core: 2. Of those that a mesh axis runs over, the one named last changes fastest.
Arguments:
- patches_in: bfloat16 [32, 256, 1152], P(('dp', 'fsdp')), may hold values from -6 to 6
- condition: bfloat16 [32, 1152], P(('dp', 'fsdp')), may hold values from -6 to 6
- keep_count: int32 [32], P(('dp', 'fsdp')), may hold values from 48 to 192, as said below
- keep_index: int32 [32, 192], P(('dp', 'fsdp')), may hold values from 0 to 255, as said below
- w_ada: bfloat16 [1152, 6912], P('dp', 'fsdp'), may hold values from -0.1875 to 0.1875
- b_ada: bfloat16 [6912], P(('dp', 'fsdp')), may hold values from -3 to 3
- w_qkv: bfloat16 [1152, 3456], P('dp', 'fsdp'), may hold values from -0.1875 to 0.1875
- qv_bias: bfloat16 [2304], P(('dp', 'fsdp')), may hold values from -3 to 3
- w_proj: bfloat16 [1152, 1152], P('dp', 'fsdp'), may hold values from -1.5 to 1.5
- w_fc1: bfloat16 [1152, 4608], P('dp', 'fsdp'), may hold values from -0.1875 to 0.1875
- fc1_bias: bfloat16 [4608], P(('dp', 'fsdp')), may hold values from -3 to 3
- w_fc2: bfloat16 [4608, 1152], P('dp', 'fsdp'), may hold values from -0.1875 to 0.1875
- out_bias: bfloat16 [2304], P(('dp', 'fsdp')), may hold values from -3 to 3
- cotangent: bfloat16 [32, 192, 1152], P(('dp', 'fsdp')), may hold values from -6 to 6
Outputs:
- block_out: bfloat16 [32, 192, 1152], P(('dp', 'fsdp'))
- grad_patches: float32 [32, 256, 1152], P(('dp', 'fsdp'))
- grad_condition: float32 [32, 1152], P(('dp', 'fsdp'))
- grad_w_ada: float32 [1152, 6912], P('dp', 'fsdp')
- grad_b_ada: float32 [6912], P(('dp', 'fsdp'))
- grad_w_qkv: float32 [1152, 3456], P('dp', 'fsdp')
- grad_qv_bias: float32 [2304], P(('dp', 'fsdp'))
- grad_w_proj: float32 [1152, 1152], P('dp', 'fsdp')
- grad_w_fc1: float32 [1152, 4608], P('dp', 'fsdp')
- grad_fc1_bias: float32 [4608], P(('dp', 'fsdp'))
- grad_w_fc2: float32 [4608, 1152], P('dp', 'fsdp')
- grad_out_bias: float32 [2304], P(('dp', 'fsdp'))
Inputs may be any that keep to these rules, and one draw needn't show every extreme that they name: `keep_count`: the first image keeps 192 tokens and the last 48. `keep_index`: the 192 entries of an image are distinct patch numbers.
All inputs are finite; a program needn't handle non-finite values.
Results may differ from a plain program's by a relative error of at most 0.017.
The roundings to bfloat16 on the way count: a program that leaves them out, or rounds other values in their place, can miss the bound.
Values may be sent and summed in bfloat16 or wider, within the bound.
A program may use at most 192 MiB of HBM per device.

v0:
```python
import math
import jax
import jax.numpy as jnp
from jax import lax
from jax.sharding import PartitionSpec as P

HEADS = 16
epsilon = 1e-06
negative = -1e30


def layer_norm(inputs):
    centred = inputs - jnp.mean(inputs, axis=-1, keepdims=True)
    rstd = lax.rsqrt(jnp.mean(centred * centred, axis=-1, keepdims=True) + epsilon)
    return (centred * rstd, rstd)


def norm_back(upstream, normed, rstd):
    return rstd * (
        upstream
        - jnp.mean(upstream, axis=-1, keepdims=True)
        - normed * jnp.mean(upstream * normed, axis=-1, keepdims=True)
    )


def swish(inputs):
    return inputs / (1.0 + jnp.exp(-inputs))


def gelu_tanh(inputs):
    return (
        0.5
        * inputs
        * (1.0 + jnp.tanh(0.7978845608028654 * (inputs + 0.044715 * inputs * inputs * inputs)))
    )


def inner_rows(left, right):
    return lax.dot_general(
        left, right, (((0,), (0,)), ((), ())), preferred_element_type=jnp.float32
    )


def times_transposed(left, right):
    return lax.dot_general(
        left, right, (((1,), (1,)), ((), ())), preferred_element_type=jnp.float32
    )


def flat_bias(collected):
    return collected.reshape(-1)


def gather_forward(w_ada, b_ada, w_qkv, qv_bias, w_proj, w_fc1, fc1_bias, w_fc2, out_bias):
    part_ada, part_qkv, part_proj, part_one, part_two, bias_ada, bias_qv, bias_one, bias_out = (
        lax.all_gather(w_ada, "fsdp", axis=1, tiled=True),
        lax.all_gather(w_qkv, "fsdp", axis=1, tiled=True),
        lax.all_gather(w_proj, "fsdp", axis=1, tiled=True),
        lax.all_gather(w_fc1, "fsdp", axis=1, tiled=True),
        lax.all_gather(w_fc2, "fsdp", axis=1, tiled=True),
        lax.all_gather(b_ada.reshape(1, 1, -1), "fsdp", axis=1, tiled=True),
        lax.all_gather(qv_bias.reshape(1, 1, -1), "fsdp", axis=1, tiled=True),
        lax.all_gather(fc1_bias.reshape(1, 1, -1), "fsdp", axis=1, tiled=True),
        lax.all_gather(out_bias.reshape(1, 1, -1), "fsdp", axis=1, tiled=True),
    )
    gathered = (
        lax.all_gather(part_ada, "dp", axis=0, tiled=True),
        lax.all_gather(part_qkv, "dp", axis=0, tiled=True),
        lax.all_gather(part_proj, "dp", axis=0, tiled=True),
        lax.all_gather(part_one, "dp", axis=0, tiled=True),
        lax.all_gather(part_two, "dp", axis=0, tiled=True),
        lax.all_gather(bias_ada, "dp", axis=0, tiled=True),
        lax.all_gather(bias_qv, "dp", axis=0, tiled=True),
        lax.all_gather(bias_one, "dp", axis=0, tiled=True),
        lax.all_gather(bias_out, "dp", axis=0, tiled=True),
    )
    return (
        gathered[0],
        flat_bias(gathered[5]),
        gathered[1],
        flat_bias(gathered[6]),
        gathered[2],
        gathered[3],
        flat_bias(gathered[7]),
        gathered[4],
        flat_bias(gathered[8]),
    )


def gather_backward(w_ada, w_qkv, w_proj, w_fc1, w_fc2):
    part_ada, part_qkv, part_proj, part_one, part_two = (
        lax.all_gather(w_ada, "fsdp", axis=1, tiled=True),
        lax.all_gather(w_qkv, "fsdp", axis=1, tiled=True),
        lax.all_gather(w_proj, "fsdp", axis=1, tiled=True),
        lax.all_gather(w_fc1, "fsdp", axis=1, tiled=True),
        lax.all_gather(w_fc2, "fsdp", axis=1, tiled=True),
    )
    return (
        lax.all_gather(part_ada, "dp", axis=0, tiled=True),
        lax.all_gather(part_qkv, "dp", axis=0, tiled=True),
        lax.all_gather(part_proj, "dp", axis=0, tiled=True),
        lax.all_gather(part_one, "dp", axis=0, tiled=True),
        lax.all_gather(part_two, "dp", axis=0, tiled=True),
    )


def split_bias(term):
    return term.reshape(lax.axis_size("dp"), lax.axis_size("fsdp"), -1)


def own_bias(summed):
    return lax.dynamic_index_in_dim(summed, lax.axis_index("dp"), 0, keepdims=False).reshape(-1)


def owned_columns(matrix, width):
    return lax.dynamic_slice_in_dim(matrix, lax.axis_index("dp") * width, width, 1)


def column_totals(matrix):
    return jnp.sum(matrix.astype(jnp.float32), axis=0)


def shards(
    patches_in,
    condition,
    keep_count,
    keep_index,
    w_ada,
    b_ada,
    w_qkv,
    qv_bias,
    w_proj,
    w_fc1,
    fc1_bias,
    w_fc2,
    out_bias,
    cotangent,
):
    images, kept_slots = keep_index.shape
    features = patches_in.shape[2]
    hidden_units = w_fc2.shape[0] * lax.axis_size("dp")
    all_rows = images * kept_slots
    head_size = features // HEADS
    factor = 1.0 / math.sqrt(head_size)
    head_shape = (images, kept_slots, HEADS, head_size)
    row_width = features // lax.axis_size("dp")
    unit_width = hidden_units // lax.axis_size("dp")
    ada_full, ada_bias, qkv_full, qv_full, proj_full, one_full, one_bias, two_full, out_full = (
        gather_forward(w_ada, b_ada, w_qkv, qv_bias, w_proj, w_fc1, fc1_bias, w_fc2, out_bias)
    )
    inputs = patches_in.astype(jnp.float32)
    kept_in = jnp.take_along_axis(inputs, keep_index[:, :, None], axis=1)
    allowed = (jnp.arange(kept_slots)[None, :] < keep_count[:, None])[:, None, None, :]
    cond_float = condition.astype(jnp.float32)
    signal = swish(cond_float).astype(jnp.bfloat16)
    modulation = jnp.dot(signal, ada_full, preferred_element_type=jnp.float32) + ada_bias.astype(
        jnp.float32
    )
    shift_one, scale_one, gate_one, shift_two, scale_two, gate_two = [
        modulation[:, None, column * features : (column + 1) * features] for column in range(6)
    ]
    normed_one, rstd_one = layer_norm(kept_in)
    hidden_one = (
        (normed_one * (1.0 + scale_one) + shift_one)
        .astype(jnp.bfloat16)
        .reshape(all_rows, features)
    )
    qv_float = qv_full.astype(jnp.float32)
    qkv_bias = jnp.concatenate(
        [qv_float[:features], jnp.zeros((features,), jnp.float32), qv_float[features:]]
    )
    projected = (
        jnp.dot(hidden_one, qkv_full, preferred_element_type=jnp.float32) + qkv_bias
    ).astype(jnp.bfloat16)
    queries = projected[:, :features].reshape(head_shape)
    key_rows = projected[:, features : 2 * features].reshape(head_shape)
    values = projected[:, 2 * features :].reshape(head_shape)
    scores = (
        jnp.einsum("iqhe,ikhe->ihqk", queries, key_rows, preferred_element_type=jnp.float32)
        * factor
    )
    scores = jnp.where(allowed, scores, negative)
    top_score = jnp.max(scores, axis=-1, keepdims=True)
    exponent = jnp.exp(scores - top_score)
    row_total = jnp.sum(exponent, axis=-1, keepdims=True)
    log_total = top_score + jnp.log(row_total)
    softmax_low = (exponent / row_total).astype(jnp.bfloat16)
    mixed = jnp.einsum("ihqk,ikhe->iqhe", softmax_low, values, preferred_element_type=jnp.float32)
    mixed_low = mixed.reshape(all_rows, features).astype(jnp.bfloat16)
    out_float = out_full.astype(jnp.float32)
    attended = (
        jnp.dot(mixed_low, proj_full, preferred_element_type=jnp.float32) + out_float[:features]
    ).reshape(images, kept_slots, features)
    middle = kept_in + gate_one * attended
    normed_two, rstd_two = layer_norm(middle)
    hidden_two = (
        (normed_two * (1.0 + scale_two) + shift_two)
        .astype(jnp.bfloat16)
        .reshape(all_rows, features)
    )
    raised = jnp.dot(hidden_two, one_full, preferred_element_type=jnp.float32) + one_bias.astype(
        jnp.float32
    )
    activated = gelu_tanh(raised).astype(jnp.bfloat16)
    branch = (
        jnp.dot(activated, two_full, preferred_element_type=jnp.float32) + out_float[features:]
    ).reshape(images, kept_slots, features)
    block_out = (middle + gate_two * branch).astype(jnp.bfloat16)
    ada_back, qkv_back, proj_back, one_back, two_back = gather_backward(
        w_ada, w_qkv, w_proj, w_fc1, w_fc2
    )
    upstream = cotangent.astype(jnp.float32)
    d_gate_two = jnp.sum(upstream * branch, axis=1)
    d_branch = (gate_two * upstream).reshape(all_rows, features).astype(jnp.bfloat16)
    d_activated = times_transposed(d_branch, two_back)
    unused, gelu_pull = jax.vjp(gelu_tanh, raised)
    d_raised = gelu_pull(d_activated)[0].astype(jnp.bfloat16)
    d_hidden_two = times_transposed(d_raised, one_back).reshape(images, kept_slots, features)
    d_shift_two = jnp.sum(d_hidden_two, axis=1)
    d_scale_two = jnp.sum(d_hidden_two * normed_two, axis=1)
    d_middle = upstream + norm_back(d_hidden_two * (1.0 + scale_two), normed_two, rstd_two)
    d_gate_one = jnp.sum(d_middle * attended, axis=1)
    d_attended = (gate_one * d_middle).reshape(all_rows, features).astype(jnp.bfloat16)
    d_mixed = times_transposed(d_attended, proj_back).astype(jnp.bfloat16).reshape(head_shape)
    scores_again = (
        jnp.einsum("iqhe,ikhe->ihqk", queries, key_rows, preferred_element_type=jnp.float32)
        * factor
    )
    scores_again = jnp.where(allowed, scores_again, negative)
    softmax_again = jnp.exp(scores_again - log_total)
    d_softmax = jnp.einsum("iqhe,ikhe->ihqk", d_mixed, values, preferred_element_type=jnp.float32)
    row_delta = jnp.sum(d_softmax * softmax_again, axis=-1, keepdims=True)
    d_scores = (softmax_again * (d_softmax - row_delta)).astype(jnp.bfloat16)
    d_queries = (
        jnp.einsum("ihqk,ikhe->iqhe", d_scores, key_rows, preferred_element_type=jnp.float32)
        * factor
    )
    d_keys = (
        jnp.einsum("ihqk,iqhe->ikhe", d_scores, queries, preferred_element_type=jnp.float32)
        * factor
    )
    d_values = jnp.einsum(
        "ihqk,iqhe->ikhe",
        softmax_again.astype(jnp.bfloat16),
        d_mixed,
        preferred_element_type=jnp.float32,
    )
    d_projected = jnp.concatenate(
        [
            d_queries.reshape(all_rows, features),
            d_keys.reshape(all_rows, features),
            d_values.reshape(all_rows, features),
        ],
        axis=1,
    ).astype(jnp.bfloat16)
    d_hidden_one = times_transposed(d_projected, qkv_back).reshape(images, kept_slots, features)
    d_shift_one = jnp.sum(d_hidden_one, axis=1)
    d_scale_one = jnp.sum(d_hidden_one * normed_one, axis=1)
    d_kept = d_middle + norm_back(d_hidden_one * (1.0 + scale_one), normed_one, rstd_one)
    grad_patches = jnp.zeros_like(inputs).at[jnp.arange(images)[:, None], keep_index].add(d_kept)
    d_modulation = jnp.concatenate(
        [d_shift_one, d_scale_one, d_gate_one, d_shift_two, d_scale_two, d_gate_two], axis=1
    ).astype(jnp.bfloat16)
    d_signal = times_transposed(d_modulation, ada_back)
    unused_too, swish_pull = jax.vjp(swish, cond_float)
    grad_condition = swish_pull(d_signal)[0]
    piece_one = lax.all_gather(hidden_one, "dp", axis=0, tiled=True)
    piece_proj_d = lax.all_gather(d_projected, "dp", axis=0, tiled=True)
    piece_mixed = lax.all_gather(mixed_low, "dp", axis=0, tiled=True)
    piece_att_d = lax.all_gather(d_attended, "dp", axis=0, tiled=True)
    piece_two = lax.all_gather(hidden_two, "dp", axis=0, tiled=True)
    piece_raised_d = lax.all_gather(d_raised, "dp", axis=0, tiled=True)
    piece_act = lax.all_gather(activated, "dp", axis=0, tiled=True)
    piece_branch_d = lax.all_gather(d_branch, "dp", axis=0, tiled=True)
    grad_qkv = inner_rows(owned_columns(piece_one, row_width), piece_proj_d)
    grad_proj = inner_rows(owned_columns(piece_mixed, row_width), piece_att_d)
    grad_one = inner_rows(owned_columns(piece_two, row_width), piece_raised_d)
    grad_two = inner_rows(owned_columns(piece_act, unit_width), piece_branch_d)
    qkv_sums = column_totals(piece_proj_d)
    proj_sums = column_totals(piece_att_d)
    one_sums = column_totals(piece_raised_d)
    two_sums = column_totals(piece_branch_d)
    piece_signal = lax.all_gather(signal, "dp", axis=0, tiled=True)
    piece_mod_d = lax.all_gather(d_modulation, "dp", axis=0, tiled=True)
    grad_ada = inner_rows(owned_columns(piece_signal, row_width), piece_mod_d)
    ada_sums = column_totals(piece_mod_d)
    grad_qv = jnp.concatenate([qkv_sums[:features], qkv_sums[2 * features :]])
    grad_out = jnp.concatenate([proj_sums, two_sums])
    terms = (
        grad_ada,
        grad_qkv,
        grad_proj,
        grad_one,
        grad_two,
        split_bias(ada_sums),
        split_bias(grad_qv),
        split_bias(one_sums),
        split_bias(grad_out),
    )
    (
        final_ada,
        final_qkv,
        final_proj,
        final_one,
        final_two,
        final_ada_bias,
        final_qv,
        final_bias,
        final_out,
    ) = (
        lax.psum_scatter(
            terms[0].astype(jnp.bfloat16), "fsdp", scatter_dimension=1, tiled=True
        ).astype(jnp.float32),
        lax.psum_scatter(
            terms[1].astype(jnp.bfloat16), "fsdp", scatter_dimension=1, tiled=True
        ).astype(jnp.float32),
        lax.psum_scatter(
            terms[2].astype(jnp.bfloat16), "fsdp", scatter_dimension=1, tiled=True
        ).astype(jnp.float32),
        lax.psum_scatter(
            terms[3].astype(jnp.bfloat16), "fsdp", scatter_dimension=1, tiled=True
        ).astype(jnp.float32),
        lax.psum_scatter(
            terms[4].astype(jnp.bfloat16), "fsdp", scatter_dimension=1, tiled=True
        ).astype(jnp.float32),
        lax.psum_scatter(
            terms[5].astype(jnp.bfloat16), "fsdp", scatter_dimension=1, tiled=True
        ).astype(jnp.float32),
        lax.psum_scatter(
            terms[6].astype(jnp.bfloat16), "fsdp", scatter_dimension=1, tiled=True
        ).astype(jnp.float32),
        lax.psum_scatter(
            terms[7].astype(jnp.bfloat16), "fsdp", scatter_dimension=1, tiled=True
        ).astype(jnp.float32),
        lax.psum_scatter(
            terms[8].astype(jnp.bfloat16), "fsdp", scatter_dimension=1, tiled=True
        ).astype(jnp.float32),
    )
    return (
        block_out,
        grad_patches,
        grad_condition,
        final_ada,
        own_bias(final_ada_bias),
        final_qkv,
        own_bias(final_qv),
        final_proj,
        final_one,
        own_bias(final_bias),
        final_two,
        own_bias(final_out),
    )


def solution(mesh):
    placed = (
        P(("dp", "fsdp"), None, None),
        P(("dp", "fsdp"), None),
        P(("dp", "fsdp")),
        P(("dp", "fsdp"), None),
        P("dp", "fsdp"),
        P(("dp", "fsdp")),
        P("dp", "fsdp"),
        P(("dp", "fsdp")),
        P("dp", "fsdp"),
        P("dp", "fsdp"),
        P(("dp", "fsdp")),
        P("dp", "fsdp"),
        P(("dp", "fsdp")),
        P(("dp", "fsdp"), None, None),
    )
    return jax.shard_map(
        shards,
        mesh=mesh,
        in_specs=placed,
        out_specs=(
            P(("dp", "fsdp"), None, None),
            P(("dp", "fsdp"), None, None),
            P(("dp", "fsdp"), None),
            P("dp", "fsdp"),
            P(("dp", "fsdp")),
            P("dp", "fsdp"),
            P(("dp", "fsdp")),
            P("dp", "fsdp"),
            P("dp", "fsdp"),
            P(("dp", "fsdp")),
            P("dp", "fsdp"),
            P(("dp", "fsdp")),
        ),
        check_vma=False,
    )
```

profile of v0, /device:TPU:0, one launch (start us, length us, event | category | flops | bytes accessed | tf_op | source)
XLA Modules:
  0.0 1289.4 jit_solution(15727656072078803900)
XLA Ops:
  10.0 75.5 %all-gather.57.cloned.1.call-done = bf16[8,864,288]{1,2,0:T(8,128)(2,1)} async-done(((bf16[1,864,288]{1,2,0:T(8,128)(2,1)}), bf16[8,864,288]{1,2,0:T(8,128)(2,1)}) %all-gather.57.cloned.1.call-update) | async-done | bytes 3981328 | tf_op jit(solution)/shard_map/all_gather | solution.py:56
  85.5 5.5 copy.85
  91.0 7.8 reshape.741
  98.8 39.3 %all-gather.59.cloned.1.call-done = bf16[8,432,288]{1,2,0:T(8,128)(2,1)} async-done(((bf16[1,432,288]{1,2,0:T(8,128)(2,1)}), bf16[8,432,288]{1,2,0:T(8,128)(2,1)}) %all-gather.59.cloned.1.call-update) | async-done | bytes 1990672 | tf_op jit(solution)/shard_map/all_gather | solution.py:57
  138.1 3.0 copy.86
  141.1 4.0 reshape.743
  145.2 34.0 %all_gather.102 = bf16[288,1152]{0,1:T(8,128)(2,1)S(1)} all-gather(bf16[288,144]{0,1:T(8,128)(2,1)S(1)} %copy-done.19), channel_id=1, replica_groups=mesh['dp'=4,'fsdp'=8] {'fsdp'}, dimensions={1}, use_global_device_ids=true | all-gather | bytes 746496 | tf_op jit(solution)/shard_map/all_gather | solution.py:58
  180.3 23.3 %all-gather.61.cloned.1.call-done = bf16[8,576,288]{1,2,0:T(8,128)(2,1)} async-done(((bf16[1,576,288]{1,2,0:T(8,128)(2,1)}), bf16[8,576,288]{1,2,0:T(8,128)(2,1)}) %all-gather.61.cloned.1.call-update) | async-done | bytes 2654224 | tf_op jit(solution)/shard_map/all_gather | solution.py:59
  203.6 2.8 copy.92
  206.4 3.2 reshape.745
  209.8 50.1 %all-gather.37.cloned.1.call-done = bf16[1152,1152]{0,1:T(8,128)(2,1)} async-done(((bf16[1152,144]{0,1:T(8,128)(2,1)}), bf16[1152,1152]{0,1:T(8,128)(2,1)}) %all-gather.37.cloned.1.call-update) | async-done | bytes 2654224 | tf_op jit(solution)/shard_map/all_gather | solution.py:60
  263.6 34.7 %all-reduce.10 = (bf16[1728]{0:T(1024)(128)(2,1)S(1)}, bf16[576]{0:T(1024)(128)(2,1)S(1)}, bf16[576]{0:T(1024)(128)(2,1)S(1)}, bf16[1152]{0:T(1024)(128)(2,1)S(1)}) all-reduce(bf16[1728]{0:T(1024)(128)(2,1)S(1)} %dynamic-update-slice, bf16[576]{0:T(1024)(128)(2,1)S(1)} %dynamic-update-slice.1, ...), channel_id=2, replica_groups=mesh['dp'=4,'fsdp'=8] {'fsdp'}, use_global_device_ids=true, to_apply=%add.1 | all-reduce | flops 4032 | bytes 16128
  298.4 5.2 all_gather.109
  303.8 5.2 all_gather.97
  309.2 5.2 all_gather.105
  314.6 5.3 all_gather.101
  322.6 38.6 %all-gather.29.cloned.1.call-done = bf16[1152,6912]{1,0:T(8,128)(2,1)} async-done(((bf16[288,6912]{1,0:T(8,128)(2,1)}), bf16[1152,6912]{1,0:T(8,128)(2,1)}) %all-gather.29.cloned.1.call-update) | async-done | bytes 15925264 | tf_op jit(solution)/shard_map/all_gather | solution.py:67
  361.2 7.7 convolution_reduce_fusion
  369.4 49.2 %all-gather.31.cloned.1.call-done = bf16[1152,3456]{1,0:T(8,128)(2,1)} async-done(((bf16[288,3456]{1,0:T(8,128)(2,1)}), bf16[1152,3456]{1,0:T(8,128)(2,1)}) %all-gather.31.cloned.1.call-update) | async-done | bytes 7962640 | tf_op jit(solution)/shard_map/all_gather | solution.py:68
  418.6 5.2 fusion
  427.1 2.3 fusion.70
  431.4 15.1 %all-gather.33.cloned.1.call-done = bf16[1152,1152]{1,0:T(8,128)(2,1)} async-done(((bf16[288,1152]{1,0:T(8,128)(2,1)}), bf16[1152,1152]{1,0:T(8,128)(2,1)}) %all-gather.33.cloned.1.call-update) | async-done | bytes 2654224 | tf_op jit(solution)/shard_map/all_gather | solution.py:69
  446.5 4.0 fusion.64
  452.5 2.2 add_convert_fusion.1
  454.7 64.3 %all-gather.35.cloned.1.call-done = bf16[1152,4608]{1,0:T(8,128)(2,1)} async-done(((bf16[288,4608]{1,0:T(8,128)(2,1)}), bf16[1152,4608]{1,0:T(8,128)(2,1)}) %all-gather.35.cloned.1.call-update) | async-done | bytes 10616848 | tf_op jit(solution)/shard_map/all_gather | solution.py:70
  519.0 9.5 multiply_convert_fusion
  528.6 63.0 %all-gather.39.cloned.1.call-done = bf16[4608,1152]{0,1:T(8,128)(2,1)} async-done(((bf16[1152,1152]{0,1:T(8,128)(2,1)}), bf16[4608,1152]{0,1:T(8,128)(2,1)}) %all-gather.39.cloned.1.call-update) | async-done | bytes 10616848 | tf_op jit(solution)/shard_map/all_gather | solution.py:71
  591.5 8.4 fusion.4
  599.9 9.1 fusion.71
  609.0 8.3 convolution_add_fusion.3
  621.1 2.1 copy.102
  623.8 3.7 convolution_convert_fusion.5
  627.5 2.1 copy.93
  629.6 2.5 fusion.17
  632.1 2.1 copy.99
  634.2 2.1 multiply_reduce_fusion
  645.1 7.4 multiply_reduce_fusion.2
  654.0 10.4 convert_bitcast_fusion
  664.4 5.2 all-gather.9
  669.6 4.0 convolution_convert_fusion.4
  673.8 6.0 all-gather.10
  680.4 3.2 convolution_convert_fusion
  683.6 6.6 copy.109
  690.2 39.4 %all-gather.43.cloned.1.call-done = bf16[768,3456]{1,0:T(8,128)(2,1)} async-done(((bf16[192,3456]{1,0:T(8,128)(2,1)}), bf16[768,3456]{1,0:T(8,128)(2,1)}) %all-gather.43.cloned.1.call-update) | async-done | bytes 5308432 | tf_op jit(solution)/shard_map/all_gather | solution.py:268
  729.6 4.7 convolution_convert_fusion.3
  734.3 2.7 copy.111
  737.2 14.6 %all-gather.47.cloned.1.call-done = bf16[768,1152]{1,0:T(8,128)(2,1)} async-done(((bf16[192,1152]{1,0:T(8,128)(2,1)}), bf16[768,1152]{1,0:T(8,128)(2,1)}) %all-gather.47.cloned.1.call-update) | async-done | bytes 1769488 | tf_op jit(solution)/shard_map/all_gather | solution.py:271
  751.8 52.3 %all-gather.49.cloned.1.call-done = bf16[768,4608]{1,0:T(8,128)(2,1)} async-done(((bf16[192,4608]{1,0:T(8,128)(2,1)}), bf16[768,4608]{1,0:T(8,128)(2,1)}) %all-gather.49.cloned.1.call-update) | async-done | bytes 7077904 | tf_op jit(solution)/shard_map/all_gather | solution.py:272
  804.1 5.6 convolution_convert_fusion.2
  809.7 3.1 copy.113
  812.9 13.4 %all-gather.55.cloned.1.call-done = bf16[1,768,1152]{2,1,0:T(8,128)(2,1)} async-done(((bf16[1,192,1152]{2,1,0:T(8,128)(2,1)}), bf16[1,768,1152]{2,1,0:T(8,128)(2,1)}) %all-gather.55.cloned.1.call-update) | async-done | bytes 1769488 | tf_op jit(solution)/shard_map/all_gather | solution.py:274
  826.3 52.3 %all-gather.51.cloned.1.call-done = bf16[768,4608]{1,0:T(8,128)(2,1)} async-done(((bf16[192,4608]{1,0:T(8,128)(2,1)}), bf16[768,4608]{1,0:T(8,128)(2,1)}) %all-gather.51.cloned.1.call-update) | async-done | bytes 7077904 | tf_op jit(solution)/shard_map/all_gather | solution.py:273
  878.6 6.1 convolution_convert_fusion.1
  893.1 4.3 scatter_custom_fusion
  897.4 1.8 reduce.34
  899.7 43.4 %reduce-scatter.12.cloned.1.call-done = bf16[288,144]{0,1:T(8,128)(2,1)} async-done(((bf16[288,1152]{0,1:T(8,128)(2,1)}), bf16[288,144]{0,1:T(8,128)(2,1)}) %reduce-scatter.12.cloned.1.call-update) | async-done | bytes 82960 | tf_op jit(solution)/shard_map/reduce_scatter | solution.py:317
  944.7 105.2 %reduce-scatter.16.cloned.1.call-done = bf16[864,288]{1,0:T(8,128)(2,1)} async-done(((bf16[6912,288]{1,0:T(8,128)(2,1)}), bf16[864,288]{1,0:T(8,128)(2,1)}) %reduce-scatter.16.cloned.1.call-update) | async-done | bytes 497680
  1052.2 3.3 reduce.32
  1055.8 4.2 reduce_sum.213
  1060.1 37.4 %all-reduce.9 = (bf16[4,8,216]{2,0,1:T(4,128)(2,1)S(1)}, bf16[4,8,72]{2,0,1:T(4,128)(2,1)S(1)}, bf16[4,8,144]{2,0,1:T(4,128)(2,1)S(1)}, bf16[4,8,72]{2,0,1:T(4,128)(2,1)S(1)}) all-reduce(bf16[4,8,216]{2,0,1:T(4,128)(2,1)S(1)} %copy-done.20, bf16[4,8,72]{2,0,1:T(4,128)(2,1)S(1)} %copy.101, ...), channel_id=9, replica_groups=mesh['dp'=4,'fsdp'=8] {'fsdp'}, use_global_device_ids=true, to_apply=%region_20.21.clone | all-reduce | flops 16128 | bytes 64512
  1102.4 22.3 %reduce-scatter.18.cloned.1.call-done = bf16[432,288]{1,0:T(8,128)(2,1)} async-done(((bf16[3456,288]{1,0:T(8,128)(2,1)}), bf16[432,288]{1,0:T(8,128)(2,1)}) %reduce-scatter.18.cloned.1.call-update) | async-done | bytes 248848
  1126.7 79.7 %reduce-scatter.20.cloned.1.call-done = bf16[576,288]{1,0:T(8,128)(2,1)} async-done(((bf16[4608,288]{1,0:T(8,128)(2,1)}), bf16[576,288]{1,0:T(8,128)(2,1)}) %reduce-scatter.20.cloned.1.call-update) | async-done | bytes 331792
  1208.5 71.9 %reduce-scatter.14.cloned.1.call-done = bf16[1152,144]{0,1:T(8,128)(2,1)} async-done(((bf16[1152,1152]{0,1:T(8,128)(2,1)}), bf16[1152,144]{0,1:T(8,128)(2,1)}) %reduce-scatter.14.cloned.1.call-update) | async-done | bytes 331792 | tf_op jit(solution)/shard_map/reduce_scatter | solution.py:323
  1280.5 1.9 convert_element_type.218
  (212 shorter events, 53.9 us)
Async XLA Ops:
  7.2 78.3 %all-gather.57.cloned.1.call-start = ((), (), s32[]{:S(2)}) async-start(), calls=%async_computation.21 | async-start | bytes 4644864 | tf_op jit(solution)/shard_map/all_gather | solution.py:56
  7.9 130.2 %all-gather.59.cloned.1.call-start = ((), (), s32[]{:S(2)}) async-start(), calls=%async_computation.22 | async-start | bytes 2654208 | tf_op jit(solution)/shard_map/all_gather | solution.py:57
  8.7 194.9 %all-gather.61.cloned.1.call-start = ((), (), s32[]{:S(2)}) async-start(), calls=%async_computation.23 | async-start | bytes 3317760 | tf_op jit(solution)/shard_map/all_gather | solution.py:59
  9.4 250.5 %all-gather.37.cloned.1.call-start = ((), (), s32[]{:S(2)}) async-start(), calls=%async_computation.9 | async-start | bytes 2985984 | tf_op jit(solution)/shard_map/all_gather | solution.py:60
  10.0 351.3 %all-gather.29.cloned.1.call-start = ((), (), s32[]{:S(2)}) async-start(), calls=%async_computation.5 | async-start | bytes 19906560 | tf_op jit(solution)/shard_map/all_gather | solution.py:67
  98.8 319.8 %all-gather.31.cloned.1.call-start = ((), (), s32[]{:S(2)}) async-start(), calls=%async_computation.6 | async-start | bytes 9953280 | tf_op jit(solution)/shard_map/all_gather | solution.py:68
  141.1 4.1 copy-start.19
  145.1 301.4 %all-gather.33.cloned.1.call-start = ((), (), s32[]{:S(2)}) async-start(), calls=%async_computation.7 | async-start | bytes 3317760 | tf_op jit(solution)/shard_map/all_gather | solution.py:69
  180.3 338.7 %all-gather.35.cloned.1.call-start = ((), (), s32[]{:S(2)}) async-start(), calls=%async_computation.8 | async-start | bytes 13271040 | tf_op jit(solution)/shard_map/all_gather | solution.py:70
  209.6 50.3 %copy-start.24 = (u32[32]{0:T(128)S(1)}, u32[32]{0:T(128)}, u32[]{:S(2)}) copy-start(u32[32]{0:T(128)} %constant.100) | copy-start | bytes 388
  209.6 52.9 %copy-start.25 = (bf16[72]{0:T(256)(128)(2,1)S(1)}, bf16[72]{0:T(256)(128)(2,1)}, u32[]{:S(2)}) copy-start(bf16[72]{0:T(256)(128)(2,1)} %param.21) | copy-start | bytes 436
  209.6 53.2 %copy-start.26 = (bf16[72]{0:T(256)(128)(2,1)S(1)}, bf16[72]{0:T(256)(128)(2,1)}, u32[]{:S(2)}) copy-start(bf16[72]{0:T(256)(128)(2,1)} %param.26) | copy-start | bytes 436
  209.7 53.4 %copy-start.27 = (bf16[216]{0:T(256)(128)(2,1)S(1)}, bf16[216]{0:T(256)(128)(2,1)}, u32[]{:S(2)}) copy-start(bf16[216]{0:T(256)(128)(2,1)} %param.19) | copy-start | bytes 1300
  209.7 53.7 %copy-start.28 = (bf16[144]{0:T(256)(128)(2,1)S(1)}, bf16[144]{0:T(256)(128)(2,1)}, u32[]{:S(2)}) copy-start(bf16[144]{0:T(256)(128)(2,1)} %param.24) | copy-start | bytes 868
  209.7 111.2 %copy-start.23 = (s32[1,192]{1,0:T(1,128)S(1)}, s32[1,192]{1,0:T(1,128)}, u32[]{:S(2)}) copy-start(s32[1,192]{1,0:T(1,128)} %param.17) | copy-start | bytes 2308
  209.7 111.2 %copy-start.18 = (bf16[1,256,1152]{2,1,0:T(8,128)(2,1)S(1)}, bf16[1,256,1152]{2,1,0:T(8,128)(2,1)}, u32[]{:S(2)}) copy-start(bf16[1,256,1152]{2,1,0:T(8,128)(2,1)} %param.14) | copy-start | bytes 1769476
  209.7 381.8 %all-gather.39.cloned.1.call-start = ((), (), s32[]{:S(2)}) async-start(), calls=%async_computation.10 | async-start | bytes 13271040 | tf_op jit(solution)/shard_map/all_gather | solution.py:71
  259.9 409.7 %all-gather.53.cloned.1.call-start = ((), (), s32[]{:S(2)}) async-start(), calls=%async_computation.19 | async-start | bytes 2211840 | tf_op jit(solution)/shard_map/all_gather | solution.py:270
  321.0 40.3 %copy-start.21 = (bf16[1,1152]{1,0:T(2,128)(2,1)S(1)}, bf16[1,1152]{1,0:T(2,128)(2,1)}, u32[]{:S(2)}) copy-start(bf16[1,1152]{1,0:T(2,128)(2,1)} %param.15) | copy-start | bytes 6916
  322.0 47.1 %copy-start = (f32[192,1152]{1,0:T(8,128)}, f32[192,1152]{1,0:T(8,128)S(1)}, u32[]{:S(2)}) copy-start(f32[192,1152]{1,0:T(8,128)S(1)} %gather_fusion) | copy-start | bytes 2654212
  322.6 322.4 %copy-start.22 = (f32[192]{0:T(256)}, f32[192]{0:T(256)S(1)}, u32[]{:S(2)}) copy-start(f32[192]{0:T(256)S(1)} %add_rsqrt_fusion.1) | copy-start | bytes 2308
  369.4 54.4 %copy-start.12 = (bf16[192,1152]{1,0:T(8,128)(2,1)}, bf16[192,1152]{1,0:T(8,128)(2,1)S(1)}, u32[]{:S(2)}) copy-start(bf16[192,1152]{1,0:T(8,128)(2,1)S(1)} %add_convert_fusion.2) | copy-start | bytes 1327108
  427.1 2.8 copy-start.11
  446.5 5.2 copy-start.14
  450.5 0.9 copy-start.2
  609.0 8.3 copy-start.3
  609.0 8.3 copy-start.10
  617.4 1.2 copy-start.9
  617.4 1.3 copy-start.15
  619.3 0.9 copy-start.5
  621.0 48.6 %all-gather.45.cloned.1.call-start = ((), (), s32[]{:S(2)}) async-start(), calls=%async_computation.13 | async-start | bytes 2211840 | tf_op jit(solution)/shard_map/all_gather | solution.py:269
  623.2 67.0 %all-gather.41.cloned.1.call-start = ((), (), s32[]{:S(2)}) async-start(), calls=%async_computation.11 | async-start | bytes 2211840 | tf_op jit(solution)/shard_map/all_gather | solution.py:267
  623.8 105.8 %all-gather.43.cloned.1.call-start = ((), (), s32[]{:S(2)}) async-start(), calls=%async_computation.12 | async-start | bytes 6635520 | tf_op jit(solution)/shard_map/all_gather | solution.py:268
  636.4 2.0 copy-start.8
  637.1 1.2 copy-start.4
  638.3 1.1 copy-start.7
  638.3 3.1 copy-start.16
  642.6 2.4 copy-start.1
  642.7 109.2 %all-gather.47.cloned.1.call-start = ((), (), s32[]{:S(2)}) async-start(), calls=%async_computation.15 | async-start | bytes 2211840 | tf_op jit(solution)/shard_map/all_gather | solution.py:271
  643.2 160.9 %all-gather.49.cloned.1.call-start = ((), (), s32[]{:S(2)}) async-start(), calls=%async_computation.16 | async-start | bytes 8847360 | tf_op jit(solution)/shard_map/all_gather | solution.py:272
  643.8 182.5 %all-gather.55.cloned.1.call-start = ((), (), s32[]{:S(2)}) async-start(), calls=%async_computation.20 | async-start | bytes 2211840 | tf_op jit(solution)/shard_map/all_gather | solution.py:274
  644.4 234.2 %all-gather.51.cloned.1.call-start = ((), (), s32[]{:S(2)}) async-start(), calls=%async_computation.17 | async-start | bytes 8847360 | tf_op jit(solution)/shard_map/all_gather | solution.py:273
  645.0 298.1 %reduce-scatter.12.cloned.1.call-start = ((), (), s32[]{:S(2)}) async-start(), calls=%async_computation.14 | async-start | bytes 995328 | tf_op jit(solution)/shard_map/reduce_scatter | solution.py:317
  673.6 376.2 %reduce-scatter.16.cloned.1.call-start = ((), (), s32[]{:S(2)}) async-start(), calls=%async_computation.24 | async-start | bytes 5971968
  679.7 0.6 copy-start.17
  690.1 434.5 %reduce-scatter.18.cloned.1.call-start = ((), (), s32[]{:S(2)}) async-start(), calls=%async_computation.25 | async-start | bytes 2985984
  736.9 469.5 %reduce-scatter.20.cloned.1.call-start = ((), (), s32[]{:S(2)}) async-start(), calls=%async_computation.26 | async-start | bytes 3981312
  812.8 467.6 %reduce-scatter.14.cloned.1.call-start = ((), (), s32[]{:S(2)}) async-start(), calls=%async_computation.18 | async-start | bytes 2985984 | tf_op jit(solution)/shard_map/reduce_scatter | solution.py:323
  884.7 8.3 copy-start.6
  884.7 14.5 %copy-start.13 = (bf16[1,768,1152]{2,1,0:T(8,128)(2,1)S(1)}, bf16[1,768,1152]{2,1,0:T(8,128)(2,1)}, u32[]{:S(2)}) copy-start(bf16[1,768,1152]{2,1,0:T(8,128)(2,1)} %all-gather.53.cloned.1.call-done) | copy-start | bytes 5308420
  1055.8 4.3 copy-start.20
Sparse Core Ops, SparseCore 0:
  10.2 75.2 all-gather.56
  87.7 50.3 all-gather.58
  140.3 63.2 all-gather.60
  205.6 54.2 all-gather.36
  261.3 99.9 all-gather.28
  362.7 55.8 all-gather.30
  420.7 25.7 all-gather.32
  448.0 70.9 all-gather.34
  520.6 70.8 all-gather.38
  621.2 20.8 all-gather.52
  643.6 20.7 all-gather.44
  665.8 21.3 all-gather.40
  688.8 40.7 all-gather.42
  731.0 20.7 all-gather.46
  753.2 50.8 all-gather.48
  805.5 20.7 all-gather.54
  827.7 50.8 all-gather.50
  881.9 61.1 reduce-scatter.11
  946.7 103.1 reduce-scatter.15
  1053.8 70.8 reduce-scatter.17
  1128.3 78.0 reduce-scatter.19
  1210.1 70.3 reduce-scatter.13
where the time goes:
time: 1300 us; the launch traced here: 1290 us
  waiting for transfers between devices  918 us (71%)
  blocking collectives  138 us (11%)
  matrix products  108 us (8%)
  local copies, waits for them, and re-layouts  66.9 us (5%)
  other arithmetic  38.9 us (3%)
  between operations  17.8 us (1%)
    unnamed x25, waiting for transfers between devices  212 us
    all_gather x1, waiting for transfers between devices, gather_forward(): lax.all_gather(w_ada, 'fsdp', axis=1, tiled=True)  75.5 us
    unnamed x2, blocking collectives  72.1 us
    reduce_scatter x1, waiting for transfers between devices, shards(): lax.psum_scatter(terms[4].astype(jnp.bfloat16), 'fsdp', scatter_dimension...  71.9 us
    all_gather x1, waiting for transfers between devices, gather_forward(): lax.all_gather(part_one, 'dp', axis=0, tiled=True)  64.3 us
    all_gather x1, waiting for transfers between devices, gather_forward(): lax.all_gather(part_two, 'dp', axis=0, tiled=True)  63 us
    all_gather x1, waiting for transfers between devices, shards(): piece_raised_d = lax.all_gather(d_raised, 'dp', axis=0, tiled=True)  52.3 us
    all_gather x1, waiting for transfers between devices, shards(): piece_act = lax.all_gather(activated, 'dp', axis=0, tiled=True)  52.3 us
  transfers between devices with their start and end apart: 22, of which 19 were waited for; matrix products, arithmetic and copies ran while one was open for 14% of the time, Pallas kernels for 0%

commit v1 on v0

--- a/solution.py
+++ b/solution.py
@@ -265,8 +265,11 @@
     unused_too, swish_pull = jax.vjp(swish, cond_float)
     grad_condition = swish_pull(d_signal)[0]
     piece_one = lax.all_gather(hidden_one, "dp", axis=0, tiled=True)
-    piece_proj_d = lax.all_gather(d_projected, "dp", axis=0, tiled=True)
-    piece_mixed = lax.all_gather(mixed_low, "dp", axis=0, tiled=True)
+    piece_proj_d, piece_mixed = jnp.split(
+        lax.all_gather(jnp.concatenate([d_projected, mixed_low], axis=1), "dp", axis=0, tiled=True),
+        [d_projected.shape[1]],
+        axis=1,
+    )
     piece_att_d = lax.all_gather(d_attended, "dp", axis=0, tiled=True)
     piece_two = lax.all_gather(hidden_two, "dp", axis=0, tiled=True)
     piece_raised_d = lax.all_gather(d_raised, "dp", axis=0, tiled=True)

time: 1300 us -> 1300 us (level)
    all_gather x2 -> x1, waiting for transfers between devices: 39.4 us -> 5.99 us  [shards(): lax.all_gather(jnp.concatenate([d_projected, mixed_low], axis=1), 'dp', a...]
    unnamed x25 -> x24, waiting for transfers between devices: 212 us -> 244 us
    reduce_scatter x1, waiting for transfers between devices: 43.4 us -> 13.6 us  [shards(): lax.psum_scatter(terms[2].astype(jnp.bfloat16), 'fsdp', scatter_dimension...]
    all_gather x1, waiting for transfers between devices: 0.02 us -> 22.4 us  [shards(): piece_att_d = lax.all_gather(d_attended, 'dp', axis=0, tiled=True)]
    all_gather x1, waiting for transfers between devices: 0.02 us -> 18.4 us  [shards(): piece_one = lax.all_gather(hidden_one, 'dp', axis=0, tiled=True)]
    unnamed x86 -> x110, local copies, waits for them, and re-layouts: 37.8 us -> 37.2 us
  transfers between devices with their start and end apart: 22 -> 21, of which waited for: 19 -> 21; matrix products, arithmetic and copies ran while one was open for 14% -> 12% of each run, Pallas kernels for 0% -> 0%
where the time goes in v1:
time: 1300 us; the launch traced here: 1290 us
  waiting for transfers between devices  927 us (71%)
  blocking collectives  138 us (11%)
  matrix products  106 us (8%)
  local copies, waits for them, and re-layouts  62.7 us (5%)
  other arithmetic  39.2 us (3%)
  between operations  17.9 us (1%)
    unnamed x24, waiting for transfers between devices  244 us
    all_gather x1, waiting for transfers between devices, gather_forward(): lax.all_gather(w_ada, 'fsdp', axis=1, tiled=True)  75.5 us
    reduce_scatter x1, waiting for transfers between devices, shards(): lax.psum_scatter(terms[4].astype(jnp.bfloat16), 'fsdp', scatter_dimension...  71.9 us
    unnamed x2, blocking collectives  71.4 us
    all_gather x1, waiting for transfers between devices, gather_forward(): lax.all_gather(part_one, 'dp', axis=0, tiled=True)  64.3 us
    all_gather x1, waiting for transfers between devices, gather_forward(): lax.all_gather(part_two, 'dp', axis=0, tiled=True)  63 us
    all_gather x1, waiting for transfers between devices, shards(): piece_act = lax.all_gather(activated, 'dp', axis=0, tiled=True)  52.3 us
    all_gather x1, waiting for transfers between devices, shards(): piece_raised_d = lax.all_gather(d_raised, 'dp', axis=0, tiled=True)  52.3 us
  transfers between devices with their start and end apart: 21, of which 21 were waited for; matrix products, arithmetic and copies ran while one was open for 12% of the time, Pallas kernels for 0%

profile of v1, /device:TPU:0, one launch (start us, length us, event | category | flops | bytes accessed | tf_op | source)
XLA Modules:
  0.0 1292.3 jit_solution(7236544811198658613)
XLA Ops:
  10.0 75.5 %all-gather.54.cloned.1.call-done = bf16[8,864,288]{1,2,0:T(8,128)(2,1)} async-done(((bf16[1,864,288]{1,2,0:T(8,128)(2,1)}), bf16[8,864,288]{1,2,0:T(8,128)(2,1)}) %all-gather.54.cloned.1.call-update) | async-done | bytes 3981328 | tf_op jit(solution)/shard_map/all_gather | solution.py:56
  85.5 5.5 copy.85
  91.0 7.8 reshape.741
  98.8 39.2 %all-gather.56.cloned.1.call-done = bf16[8,432,288]{1,2,0:T(8,128)(2,1)} async-done(((bf16[1,432,288]{1,2,0:T(8,128)(2,1)}), bf16[8,432,288]{1,2,0:T(8,128)(2,1)}) %all-gather.56.cloned.1.call-update) | async-done | bytes 1990672 | tf_op jit(solution)/shard_map/all_gather | solution.py:57
  138.1 3.0 copy.86
  141.1 4.0 reshape.743
  145.2 34.1 %all_gather.99 = bf16[288,1152]{0,1:T(8,128)(2,1)S(1)} all-gather(bf16[288,144]{0,1:T(8,128)(2,1)S(1)} %copy-done.21), channel_id=1, replica_groups=mesh['dp'=4,'fsdp'=8] {'fsdp'}, dimensions={1}, use_global_device_ids=true | all-gather | bytes 746496 | tf_op jit(solution)/shard_map/all_gather | solution.py:58
  180.4 23.3 %all-gather.58.cloned.1.call-done = bf16[8,576,288]{1,2,0:T(8,128)(2,1)} async-done(((bf16[1,576,288]{1,2,0:T(8,128)(2,1)}), bf16[8,576,288]{1,2,0:T(8,128)(2,1)}) %all-gather.58.cloned.1.call-update) | async-done | bytes 2654224 | tf_op jit(solution)/shard_map/all_gather | solution.py:59
  203.7 2.8 copy.92
  206.5 3.2 reshape.745
  209.9 50.0 %all-gather.36.cloned.1.call-done = bf16[1152,1152]{0,1:T(8,128)(2,1)} async-done(((bf16[1152,144]{0,1:T(8,128)(2,1)}), bf16[1152,1152]{0,1:T(8,128)(2,1)}) %all-gather.36.cloned.1.call-update) | async-done | bytes 2654224 | tf_op jit(solution)/shard_map/all_gather | solution.py:60
  263.5 34.7 %all-reduce.10 = (bf16[1728]{0:T(1024)(128)(2,1)S(1)}, bf16[576]{0:T(1024)(128)(2,1)S(1)}, bf16[576]{0:T(1024)(128)(2,1)S(1)}, bf16[1152]{0:T(1024)(128)(2,1)S(1)}) all-reduce(bf16[1728]{0:T(1024)(128)(2,1)S(1)} %dynamic-update-slice, bf16[576]{0:T(1024)(128)(2,1)S(1)} %dynamic-update-slice.1, ...), channel_id=2, replica_groups=mesh['dp'=4,'fsdp'=8] {'fsdp'}, use_global_device_ids=true, to_apply=%add.1 | all-reduce | flops 4032 | bytes 16128
  298.4 5.2 all_gather.106
  303.8 5.2 all_gather.94
  309.2 5.2 all_gather.102
  314.6 5.3 all_gather.98
  322.6 38.7 %all-gather.28.cloned.1.call-done = bf16[1152,6912]{1,0:T(8,128)(2,1)} async-done(((bf16[288,6912]{1,0:T(8,128)(2,1)}), bf16[1152,6912]{1,0:T(8,128)(2,1)}) %all-gather.28.cloned.1.call-update) | async-done | bytes 15925264 | tf_op jit(solution)/shard_map/all_gather | solution.py:67
  361.3 7.7 convolution_reduce_fusion
  369.4 49.2 %all-gather.30.cloned.1.call-done = bf16[1152,3456]{1,0:T(8,128)(2,1)} async-done(((bf16[288,3456]{1,0:T(8,128)(2,1)}), bf16[1152,3456]{1,0:T(8,128)(2,1)}) %all-gather.30.cloned.1.call-update) | async-done | bytes 7962640 | tf_op jit(solution)/shard_map/all_gather | solution.py:68
  418.6 5.2 fusion
  427.1 2.3 fusion.77
  431.5 15.1 %all-gather.32.cloned.1.call-done = bf16[1152,1152]{1,0:T(8,128)(2,1)} async-done(((bf16[288,1152]{1,0:T(8,128)(2,1)}), bf16[1152,1152]{1,0:T(8,128)(2,1)}) %all-gather.32.cloned.1.call-update) | async-done | bytes 2654224 | tf_op jit(solution)/shard_map/all_gather | solution.py:69
  446.5 4.0 fusion.71
  452.5 2.2 add_convert_fusion.1
  454.7 64.3 %all-gather.34.cloned.1.call-done = bf16[1152,4608]{1,0:T(8,128)(2,1)} async-done(((bf16[288,4608]{1,0:T(8,128)(2,1)}), bf16[1152,4608]{1,0:T(8,128)(2,1)}) %all-gather.34.cloned.1.call-update) | async-done | bytes 10616848 | tf_op jit(solution)/shard_map/all_gather | solution.py:70
  519.1 9.5 multiply_convert_fusion
  528.6 63.0 %all-gather.38.cloned.1.call-done = bf16[4608,1152]{0,1:T(8,128)(2,1)} async-done(((bf16[1152,1152]{0,1:T(8,128)(2,1)}), bf16[4608,1152]{0,1:T(8,128)(2,1)}) %all-gather.38.cloned.1.call-update) | async-done | bytes 10616848 | tf_op jit(solution)/shard_map/all_gather | solution.py:71
  591.6 8.3 fusion.5
  599.9 9.1 fusion.78
  609.0 8.3 convolution_add_fusion.3
  621.5 3.7 convolution_convert_fusion.5
  625.2 2.1 copy.93
  627.3 2.6 fusion.24
  639.8 8.1 multiply_reduce_fusion.2
  649.4 10.4 convert_bitcast_fusion
  659.8 5.2 all-gather.9
  665.1 6.0 all-gather.10
  671.8 3.2 convolution_convert_fusion
  675.0 6.6 copy.109
  681.6 6.0 all-gather.42.cloned.1.call-done
  687.6 22.4 %all-gather.50.cloned.1.call-done = bf16[1,768,1152]{2,1,0:T(8,128)(2,1)} async-done(((bf16[1,192,1152]{2,1,0:T(8,128)(2,1)}), bf16[1,768,1152]{2,1,0:T(8,128)(2,1)}) %all-gather.50.cloned.1.call-update) | async-done | bytes 1769488 | tf_op jit(solution)/shard_map/all_gather | solution.py:273
  710.0 3.7 convolution_convert_fusion.4
  713.8 18.4 %all-gather.40.cloned.1.call-done = bf16[768,1152]{1,0:T(8,128)(2,1)} async-done(((bf16[192,1152]{1,0:T(8,128)(2,1)}), bf16[768,1152]{1,0:T(8,128)(2,1)}) %all-gather.40.cloned.1.call-update) | async-done | bytes 1769488 | tf_op jit(solution)/shard_map/all_gather | solution.py:267
  732.2 4.7 convolution_convert_fusion.3
  736.9 2.6 copy.111
  739.7 14.8 %all-gather.44.cloned.1.call-done = bf16[768,1152]{1,0:T(8,128)(2,1)} async-done(((bf16[192,1152]{1,0:T(8,128)(2,1)}), bf16[768,1152]{1,0:T(8,128)(2,1)}) %all-gather.44.cloned.1.call-update) | async-done | bytes 1769488 | tf_op jit(solution)/shard_map/all_gather | solution.py:274
  754.5 52.3 %all-gather.46.cloned.1.call-done = bf16[768,4608]{1,0:T(8,128)(2,1)} async-done(((bf16[192,4608]{1,0:T(8,128)(2,1)}), bf16[768,4608]{1,0:T(8,128)(2,1)}) %all-gather.46.cloned.1.call-update) | async-done | bytes 7077904 | tf_op jit(solution)/shard_map/all_gather | solution.py:275
  806.8 5.6 convolution_convert_fusion.2
  812.5 3.1 copy.113
  815.6 13.4 %all-gather.52.cloned.1.call-done = bf16[1,768,1152]{2,1,0:T(8,128)(2,1)} async-done(((bf16[1,192,1152]{2,1,0:T(8,128)(2,1)}), bf16[1,768,1152]{2,1,0:T(8,128)(2,1)}) %all-gather.52.cloned.1.call-update) | async-done | bytes 1769488 | tf_op jit(solution)/shard_map/all_gather | solution.py:277
  829.0 52.3 %all-gather.48.cloned.1.call-done = bf16[768,4608]{1,0:T(8,128)(2,1)} async-done(((bf16[192,4608]{1,0:T(8,128)(2,1)}), bf16[768,4608]{1,0:T(8,128)(2,1)}) %all-gather.48.cloned.1.call-update) | async-done | bytes 7077904 | tf_op jit(solution)/shard_map/all_gather | solution.py:276
  881.3 6.1 convolution_convert_fusion.1
  888.9 1.6 reduce_sum.211
  895.8 4.3 scatter_custom_fusion
  900.1 1.8 reduce.34
  902.4 86.6 %reduce-scatter.16.cloned.1.call-done = bf16[864,288]{1,0:T(8,128)(2,1)} async-done(((bf16[6912,288]{1,0:T(8,128)(2,1)}), bf16[864,288]{1,0:T(8,128)(2,1)}) %reduce-scatter.16.cloned.1.call-update) | async-done | bytes 497680
  991.4 3.3 slice_reduce_fusion
  995.0 4.2 reduce_sum.213
  999.3 36.6 %all-reduce.9 = (bf16[4,8,216]{2,0,1:T(4,128)(2,1)S(1)}, bf16[4,8,72]{2,0,1:T(4,128)(2,1)S(1)}, bf16[4,8,144]{2,0,1:T(4,128)(2,1)S(1)}, bf16[4,8,72]{2,0,1:T(4,128)(2,1)S(1)}) all-reduce(bf16[4,8,216]{2,0,1:T(4,128)(2,1)S(1)} %copy-done.22, bf16[4,8,72]{2,0,1:T(4,128)(2,1)S(1)} %copy.102, ...), channel_id=9, replica_groups=mesh['dp'=4,'fsdp'=8] {'fsdp'}, use_global_device_ids=true, to_apply=%region_20.21.clone | all-reduce | flops 16128 | bytes 64512
  1040.4 13.6 %reduce-scatter.12.cloned.1.call-done = bf16[288,144]{0,1:T(8,128)(2,1)} async-done(((bf16[288,1152]{0,1:T(8,128)(2,1)}), bf16[288,144]{0,1:T(8,128)(2,1)}) %reduce-scatter.12.cloned.1.call-update) | async-done | bytes 82960 | tf_op jit(solution)/shard_map/reduce_scatter | solution.py:320
  1055.6 72.3 %reduce-scatter.18.cloned.1.call-done = bf16[432,288]{1,0:T(8,128)(2,1)} async-done(((bf16[3456,288]{1,0:T(8,128)(2,1)}), bf16[432,288]{1,0:T(8,128)(2,1)}) %reduce-scatter.18.cloned.1.call-update) | async-done | bytes 248848
  1129.9 79.5 %reduce-scatter.20.cloned.1.call-done = bf16[576,288]{1,0:T(8,128)(2,1)} async-done(((bf16[4608,288]{1,0:T(8,128)(2,1)}), bf16[576,288]{1,0:T(8,128)(2,1)}) %reduce-scatter.20.cloned.1.call-update) | async-done | bytes 331792
  1211.5 71.9 %reduce-scatter.14.cloned.1.call-done = bf16[1152,144]{0,1:T(8,128)(2,1)} async-done(((bf16[1152,1152]{0,1:T(8,128)(2,1)}), bf16[1152,144]{0,1:T(8,128)(2,1)}) %reduce-scatter.14.cloned.1.call-update) | async-done | bytes 331792 | tf_op jit(solution)/shard_map/reduce_scatter | solution.py:326
  1283.4 1.9 convert_element_type.218
  (235 shorter events, 52.6 us)
Async XLA Ops:
  7.2 78.3 %all-gather.54.cloned.1.call-start = ((), (), s32[]{:S(2)}) async-start(), calls=%async_computation.20 | async-start | bytes 4644864 | tf_op jit(solution)/shard_map/all_gather | solution.py:56
  7.9 130.2 %all-gather.56.cloned.1.call-start = ((), (), s32[]{:S(2)}) async-start(), calls=%async_computation.21 | async-start | bytes 2654208 | tf_op jit(solution)/shard_map/all_gather | solution.py:57
  8.7 195.0 %all-gather.58.cloned.1.call-start = ((), (), s32[]{:S(2)}) async-start(), calls=%async_computation.22 | async-start | bytes 3317760 | tf_op jit(solution)/shard_map/all_gather | solution.py:59
  9.4 250.5 %all-gather.36.cloned.1.call-start = ((), (), s32[]{:S(2)}) async-start(), calls=%async_computation.9 | async-start | bytes 2985984 | tf_op jit(solution)/shard_map/all_gather | solution.py:60
  10.0 351.3 %all-gather.28.cloned.1.call-start = ((), (), s32[]{:S(2)}) async-start(), calls=%async_computation.5 | async-start | bytes 19906560 | tf_op jit(solution)/shard_map/all_gather | solution.py:67
  98.8 319.8 %all-gather.30.cloned.1.call-start = ((), (), s32[]{:S(2)}) async-start(), calls=%async_computation.6 | async-start | bytes 9953280 | tf_op jit(solution)/shard_map/all_gather | solution.py:68
  141.1 4.1 copy-start.21
  145.1 301.4 %all-gather.32.cloned.1.call-start = ((), (), s32[]{:S(2)}) async-start(), calls=%async_computation.7 | async-start | bytes 3317760 | tf_op jit(solution)/shard_map/all_gather | solution.py:69
  180.4 338.7 %all-gather.34.cloned.1.call-start = ((), (), s32[]{:S(2)}) async-start(), calls=%async_computation.8 | async-start | bytes 13271040 | tf_op jit(solution)/shard_map/all_gather | solution.py:70
  209.8 50.2 %copy-start.36 = (u32[32]{0:T(128)S(1)}, u32[32]{0:T(128)}, u32[]{:S(2)}) copy-start(u32[32]{0:T(128)} %constant.100) | copy-start | bytes 388
  209.8 52.8 %copy-start.37 = (bf16[72]{0:T(256)(128)(2,1)S(1)}, bf16[72]{0:T(256)(128)(2,1)}, u32[]{:S(2)}) copy-start(bf16[72]{0:T(256)(128)(2,1)} %param.21) | copy-start | bytes 436
  209.8 53.0 %copy-start.38 = (bf16[72]{0:T(256)(128)(2,1)S(1)}, bf16[72]{0:T(256)(128)(2,1)}, u32[]{:S(2)}) copy-start(bf16[72]{0:T(256)(128)(2,1)} %param.26) | copy-start | bytes 436
  209.8 53.3 %copy-start.39 = (bf16[216]{0:T(256)(128)(2,1)S(1)}, bf16[216]{0:T(256)(128)(2,1)}, u32[]{:S(2)}) copy-start(bf16[216]{0:T(256)(128)(2,1)} %param.19) | copy-start | bytes 1300
  209.8 53.5 %copy-start.40 = (bf16[144]{0:T(256)(128)(2,1)S(1)}, bf16[144]{0:T(256)(128)(2,1)}, u32[]{:S(2)}) copy-start(bf16[144]{0:T(256)(128)(2,1)} %param.24) | copy-start | bytes 868
  209.8 111.0 %copy-start.35 = (s32[1,192]{1,0:T(1,128)S(1)}, s32[1,192]{1,0:T(1,128)}, u32[]{:S(2)}) copy-start(s32[1,192]{1,0:T(1,128)} %param.17) | copy-start | bytes 2308
  209.8 111.1 %copy-start.20 = (bf16[1,256,1152]{2,1,0:T(8,128)(2,1)S(1)}, bf16[1,256,1152]{2,1,0:T(8,128)(2,1)}, u32[]{:S(2)}) copy-start(bf16[1,256,1152]{2,1,0:T(8,128)(2,1)} %param.14) | copy-start | bytes 1769476
  209.8 381.7 %all-gather.38.cloned.1.call-start = ((), (), s32[]{:S(2)}) async-start(), calls=%async_computation.10 | async-start | bytes 13271040 | tf_op jit(solution)/shard_map/all_gather | solution.py:71
  260.0 427.7 %all-gather.42.cloned.1.call-start = ((), (), s32[]{:S(2)}) async-start(), calls=%async_computation.12 | async-start | bytes 8847360 | tf_op jit(solution)/shard_map/all_gather | solution.py:269
  321.0 40.3 %copy-start.25 = (bf16[1,1152]{1,0:T(2,128)(2,1)S(1)}, bf16[1,1152]{1,0:T(2,128)(2,1)}, u32[]{:S(2)}) copy-start(bf16[1,1152]{1,0:T(2,128)(2,1)} %param.15) | copy-start | bytes 6916
  322.0 47.1 %copy-start = (f32[192,1152]{1,0:T(8,128)}, f32[192,1152]{1,0:T(8,128)S(1)}, u32[]{:S(2)}) copy-start(f32[192,1152]{1,0:T(8,128)S(1)} %gather_fusion) | copy-start | bytes 2654212
  322.1 124.4 %copy-start.30 = (pred[192]{0:T(512)(128)(4,1)}, pred[192]{0:T(512)(128)(4,1)S(1)}, u32[]{:S(2)}) copy-start(pred[192]{0:T(512)(128)(4,1)S(1)} %compare_and_fusion) | copy-start | bytes 580
  322.3 46.8 %copy-start.27 = (f32[192]{0:T(256)}, f32[192]{0:T(256)S(1)}, u32[]{:S(2)}) copy-start(f32[192]{0:T(256)S(1)} %broadcast_multiply_fusion.5) | copy-start | bytes 2308
  322.6 46.5 %copy-start.33 = (f32[192]{0:T(256)}, f32[192]{0:T(256)S(1)}, u32[]{:S(2)}) copy-start(f32[192]{0:T(256)S(1)} %add_rsqrt_fusion.1) | copy-start | bytes 2308
  369.4 54.4 %copy-start.15 = (bf16[192,1152]{1,0:T(8,128)(2,1)}, bf16[192,1152]{1,0:T(8,128)(2,1)S(1)}, u32[]{:S(2)}) copy-start(bf16[192,1152]{1,0:T(8,128)(2,1)S(1)} %add_convert_fusion.2) | copy-start | bytes 1327108
  427.1 2.8 copy-start.12
  446.5 5.2 copy-start.17
  450.5 0.9 copy-start.2
  609.0 8.3 copy-start.3
  609.0 8.3 copy-start.10
  617.3 1.2 copy-start.9
  617.4 1.3 copy-start.18
  619.8 0.9 copy-start.4
  627.3 2.6 copy-start.8
  627.3 2.6 copy-start.13
  630.9 1.1 copy-start.6
  631.9 1.1 copy-start.7
  631.9 1.4 copy-start.11
  631.9 1.7 copy-start.14
  635.8 3.9 copy-start.1
  635.8 3.9 copy-start.28
  635.8 3.9 copy-start.31
  635.8 3.9 copy-start.34
  635.9 74.1 %all-gather.50.cloned.1.call-start = ((), (), s32[]{:S(2)}) async-start(), calls=%async_computation.18 | async-start | bytes 2211840 | tf_op jit(solution)/shard_map/all_gather | solution.py:273
  636.6 95.6 %all-gather.40.cloned.1.call-start = ((), (), s32[]{:S(2)}) async-start(), calls=%async_computation.11 | async-start | bytes 2211840 | tf_op jit(solution)/shard_map/all_gather | solution.py:267
  637.2 117.4 %all-gather.44.cloned.1.call-start = ((), (), s32[]{:S(2)}) async-start(), calls=%async_computation.14 | async-start | bytes 2211840 | tf_op jit(solution)/shard_map/all_gather | solution.py:274
  637.9 168.9 %all-gather.46.cloned.1.call-start = ((), (), s32[]{:S(2)}) async-start(), calls=%async_computation.15 | async-start | bytes 8847360 | tf_op jit(solution)/shard_map/all_gather | solution.py:275
  638.5 190.5 %all-gather.52.cloned.1.call-start = ((), (), s32[]{:S(2)}) async-start(), calls=%async_computation.19 | async-start | bytes 2211840 | tf_op jit(solution)/shard_map/all_gather | solution.py:277
  639.1 242.3 %all-gather.48.cloned.1.call-start = ((), (), s32[]{:S(2)}) async-start(), calls=%async_computation.16 | async-start | bytes 8847360 | tf_op jit(solution)/shard_map/all_gather | solution.py:276
  639.7 349.3 %reduce-scatter.16.cloned.1.call-start = ((), (), s32[]{:S(2)}) async-start(), calls=%async_computation.23 | async-start | bytes 5971968
  639.8 8.6 copy-start.24
  639.8 9.4 copy-start.23
  639.8 9.6 copy-start.26
  671.1 0.6 copy-start.19
  681.6 372.4 %reduce-scatter.12.cloned.1.call-start = ((), (), s32[]{:S(2)}) async-start(), calls=%async_computation.13 | async-start | bytes 995328 | tf_op jit(solution)/shard_map/reduce_scatter | solution.py:320
  687.6 22.4 %slice-start = ((bf16[768,4608]{1,0:T(8,128)(2,1)}), bf16[768,1152]{1,0:T(8,128)(2,1)S(1)}, s32[]{:S(2)}) async-start(bf16[768,4608]{1,0:T(8,128)(2,1)} %all-gather.42.cloned.1.call-done), calls=%async_computation.26 | async-start | bytes 3538944 | tf_op jit(solution)/shard_map/split | solution.py:268
  713.7 414.2 %reduce-scatter.18.cloned.1.call-start = ((), (), s32[]{:S(2)}) async-start(), calls=%async_computation.24 | async-start | bytes 2985984
  739.5 469.8 %reduce-scatter.20.cloned.1.call-start = ((), (), s32[]{:S(2)}) async-start(), calls=%async_computation.25 | async-start | bytes 3981312
  815.6 467.8 %reduce-scatter.14.cloned.1.call-start = ((), (), s32[]{:S(2)}) async-start(), calls=%async_computation.17 | async-start | bytes 2985984 | tf_op jit(solution)/shard_map/reduce_scatter | solution.py:326
  815.6 80.2 %copy-start.29 = (f32[192]{0:T(256)S(1)}, f32[192]{0:T(256)}, u32[]{:S(2)}) copy-start(f32[192]{0:T(256)} %copy-done.27) | copy-start | bytes 2308
  815.6 80.1 %copy-start.32 = (pred[192]{0:T(512)(128)(4,1)S(1)}, pred[192]{0:T(512)(128)(4,1)}, u32[]{:S(2)}) copy-start(pred[192]{0:T(512)(128)(4,1)} %copy-done.30) | copy-start | bytes 580
  887.4 8.3 copy-start.5
  887.5 14.5 %copy-start.16 = (bf16[1,768,1152]{2,1,0:T(8,128)(2,1)S(1)}, bf16[1,768,1152]{2,1,0:T(8,128)(2,1)}, u32[]{:S(2)}) copy-start(bf16[1,768,1152]{2,1,0:T(8,128)(2,1)} %all-gather.50.cloned.1.call-done) | copy-start | bytes 5308420
  995.0 4.3 copy-start.22
Sparse Core Ops, SparseCore 0:
  10.2 75.2 all-gather.53
  87.7 50.3 all-gather.55
  140.3 63.3 all-gather.57
  205.7 54.1 all-gather.35
  261.3 99.9 all-gather.27
  362.7 55.8 all-gather.29
  420.8 25.7 all-gather.31
  448.1 70.9 all-gather.33
  520.6 70.8 all-gather.37
  636.0 51.6 all-gather.41
  689.2 20.7 all-gather.49
  711.4 20.7 all-gather.39
  733.7 20.7 all-gather.43
  756.0 50.8 all-gather.45
  808.2 20.7 all-gather.51
  830.4 50.8 all-gather.47
  884.8 104.1 reduce-scatter.15
  992.6 61.2 reduce-scatter.11
  1058.1 69.7 reduce-scatter.17
  1131.3 77.9 reduce-scatter.19
  1213.0 70.3 reduce-scatter.13
